TPU v7x, 256 devices: a whole 4x4x8 slice. The times are simulated.
256 devices in a mesh: table: 16 (over y_lo, x, core), tensor: 2 (over y_hi), dp: 8 (over z).
Axes of the slice: x: 4, y: 4 (y_hi: 2, y_lo: 2; y = y_hi * 2 + y_lo), z: 8, core: 2. Of those that a mesh axis runs over, the one named last changes fastest.
Arguments:
- lookup_ids: int32 [4096, 16, 16], P('dp', 'table'), may hold values from 0 to 4095
- bag_lengths: int32 [4096, 16], P('dp', 'table'), may hold values from 1 to 16
- feature_widths: int32 [16], replicated, may hold values from 32 to 256, as said below
- tables: bfloat16 [16, 4096, 256], P('table', None, 'tensor'), may hold values from -6 to 6
- w_in: bfloat16 [4096, 16384], P(None, ('table', 'tensor')), may hold values from -0.25 to 0.25
- w_out: bfloat16 [16384, 4096], P(('table', 'tensor')), may hold values from -0.1875 to 0.1875
- cotangent: bfloat16 [4096, 4096], P('dp', ('table', 'tensor')), may hold values from -6 to 6
Outputs:
- mixed_out: bfloat16 [4096, 4096], P('dp', ('table', 'tensor'))
- grad_in: float32 [4096, 16384], P('dp', ('table', 'tensor'))
- grad_out: float32 [16384, 4096], P(('table', 'tensor', 'dp'))
Inputs may be any that keep to these rules, and one draw needn't show every extreme that they name: `feature_widths`: multiples of 32; one feature has exactly 256, another exactly 32.
All inputs are finite; a program needn't handle non-finite values.
Results may differ from a plain program's by a relative error of at most 0.0056.
Values may be sent and summed in bfloat16 or wider, within the bound.
A program may use at most 128 MiB of HBM per device.

v0:
```python
import jax
import jax.numpy as jnp
from jax import lax
from jax.sharding import PartitionSpec as P


def silu_slope(preact):
    sigmoid_part = jax.nn.sigmoid(preact)
    return sigmoid_part * (1.0 + preact * (1.0 - sigmoid_part))


def pool_local(lookup, lengths, embedding):
    samples, bag_size = lookup.shape
    vocab, half_width = embedding.shape
    vocab_block = min(vocab, 512)
    in_bag = jnp.arange(bag_size)[None, :] < lengths[:, None]
    masked = jnp.where(in_bag, lookup, -1)

    def add_block(running, first_row):
        local_ids = first_row + jnp.arange(vocab_block)
        counts = jnp.sum(masked[:, :, None] == local_ids[None, None, :], axis=1).astype(
            jnp.bfloat16
        )
        table_rows = lax.dynamic_slice_in_dim(embedding, first_row, vocab_block, 0)
        return (running + jnp.dot(counts, table_rows, preferred_element_type=jnp.float32), None)

    starts = jnp.arange(vocab // vocab_block) * vocab_block
    summed, unused = lax.scan(add_block, jnp.zeros((samples, half_width), jnp.float32), starts)
    return summed / lengths[:, None].astype(jnp.float32)


def shards(lookup_ids, bag_lengths, feature_widths, tables, w_in, w_out, cotangent):
    embedding = tables[0]
    half_width = embedding.shape[1]
    summed = pool_local(lookup_ids[:, 0, :], bag_lengths[:, 0], embedding)
    own_width = lax.dynamic_index_in_dim(feature_widths, lax.axis_index("table"), 0, keepdims=False)
    positions = lax.axis_index("tensor") * half_width + jnp.arange(half_width)
    pooled = jnp.where(positions[None, :] < own_width, summed, jnp.zeros_like(summed)).astype(
        jnp.bfloat16
    )
    features = lax.all_gather(pooled, ("table", "tensor"), axis=1, tiled=True)
    preact = jnp.dot(features, w_in, preferred_element_type=jnp.float32)
    hidden = jax.nn.silu(preact).astype(jnp.bfloat16)
    partial_out = jnp.dot(hidden, w_out, preferred_element_type=jnp.float32)
    reduced = lax.psum_scatter(partial_out, ("table", "tensor"), scatter_dimension=1, tiled=True)
    mixed_out = reduced.astype(jnp.bfloat16)
    whole_grad = lax.all_gather(cotangent, ("table", "tensor"), axis=1, tiled=True)
    contract_rows = (((0,), (0,)), ((), ()))
    contract_cols = (((1,), (1,)), ((), ()))
    grad_hidden = lax.dot_general(
        whole_grad, w_out, contract_cols, preferred_element_type=jnp.float32
    )
    grad_preact = (grad_hidden * silu_slope(preact)).astype(jnp.bfloat16)
    term_in = lax.dot_general(
        features, grad_preact, contract_rows, preferred_element_type=jnp.float32
    )
    term_out = lax.dot_general(
        hidden, whole_grad, contract_rows, preferred_element_type=jnp.float32
    )
    grad_in, grad_out = (
        lax.psum_scatter(term_in, "dp", scatter_dimension=0, tiled=True),
        lax.psum_scatter(term_out, "dp", scatter_dimension=0, tiled=True),
    )
    return (mixed_out, grad_in, grad_out)


def solution(mesh):
    return jax.shard_map(
        shards,
        mesh=mesh,
        in_specs=(
            P("dp", "table", None),
            P("dp", "table"),
            P(),
            P("table", None, "tensor"),
            P(None, ("table", "tensor")),
            P(("table", "tensor"), None),
            P("dp", ("table", "tensor")),
        ),
        out_specs=(
            P("dp", ("table", "tensor")),
            P("dp", ("table", "tensor")),
            P(("table", "tensor", "dp"), None),
        ),
        check_vma=False,
    )
```

profile of v0, /device:TPU:1, one launch (start us, length us, event | category | flops | bytes accessed | tf_op | source)
XLA Modules:
  0.0 646.2 jit_solution(7221660511315152307)
XLA Ops:
  7.9 0.9 copy.11
  8.8 0.8 bitcast_select_fusion
  9.6 64.7 %while.11 = (s32[]{:T(128)}, f32[512,128]{1,0:T(8,128)S(1)}, s32[512,16]{1,0:T(8,128)S(1)}, s32[8]{0:T(128)S(1)}, bf16[4096,128]{1,0:T(8,128)(2,1)}, /*index=5*/s32[]{:T(128)}, s32[]{:T(128)}, s32[]{:T(128)}) while((s32[]{:T(128)}, f32[512,128]{1,0:T(8,128)S(1)}, s32[512,16]{1,0:T(8,128)S(1)}, s32[8]{0:T(128)S(1)}, ...), condition=%wide.region_2.3_spmd.clone, body=%wide.region_0.2_spmd.clone.sunk | while | flops 79823368 | bytes 2789533 | solution.py:28
  12.8 3.6 convert_reduce_fusion.2
  16.5 1.2 convolution_add_fusion.2
  20.9 3.6 convert_reduce_fusion.2
  24.6 1.2 convolution_add_fusion.2
  29.0 3.6 convert_reduce_fusion.2
  32.7 1.2 convolution_add_fusion.2
  37.1 3.6 convert_reduce_fusion.2
  40.7 1.2 convolution_add_fusion.2
  45.2 3.6 convert_reduce_fusion.2
  48.8 1.2 convolution_add_fusion.2
  53.3 3.6 convert_reduce_fusion.2
  56.9 1.2 convolution_add_fusion.2
  61.4 3.6 convert_reduce_fusion.2
  65.0 1.2 convolution_add_fusion.2
  69.5 3.6 convert_reduce_fusion.2
  73.1 1.2 convolution_add_fusion.2
  75.6 0.8 select_convert_fusion
  76.5 0.7 all-gather.5.cloned.1.call-update
  77.2 89.7 %all-gather.3.cloned.1.call-done = bf16[512,4096]{1,0:T(8,128)(2,1)} async-done(((bf16[512,128]{1,0:T(8,128)(2,1)}), bf16[512,4096]{1,0:T(8,128)(2,1)}) %all-gather.3.cloned.1.call-update) | async-done | bytes 4194320 | tf_op jit(solution)/shard_map/all_gather | solution.py:41
  166.9 5.9 fusion.6
  172.8 5.6 fusion.5
  178.5 74.9 %all-gather.5.cloned.1.call-done = bf16[512,4096]{1,0:T(8,128)(2,1)} async-done(((bf16[512,128]{1,0:T(8,128)(2,1)}), bf16[512,4096]{1,0:T(8,128)(2,1)}) %all-gather.5.cloned.1.call-update) | async-done | bytes 4194320 | tf_op jit(solution)/shard_map/all_gather | solution.py:47
  253.4 6.1 fusion.3
  259.6 5.7 fusion.7
  265.3 7.9 %fusion.4 = f32[512,4096]{1,0:T(8,128)} fusion(bf16[512,4096]{1,0:T(8,128)(2,1)} %all-gather.5.cloned.1.call-done, f32[512,512]{1,0:T(8,128)S(1)} %fusion.6), kind=kOutput, calls=%fused_computation.15 | convolution fusion | flops 2148794368 | bytes 13631488 | tf_op jit(solution)/shard_map/dot_general | solution.py:57
  273.2 170.3 %reduce-scatter.4.cloned.1.call-done = f32[512,128]{1,0:T(8,128)} async-done(((f32[512,4096]{1,0:T(8,128)}), f32[512,128]{1,0:T(8,128)}) %reduce-scatter.4.cloned.1.call-update) | async-done | bytes 262160 | tf_op jit(solution)/shard_map/reduce_scatter | solution.py:45
  443.6 1.6 convert_element_type.24
  445.2 97.9 %reduce-scatter.6.cloned.1.call-done = f32[512,512]{1,0:T(8,128)} async-done(((f32[4096,512]{1,0:T(8,128)}), f32[512,512]{1,0:T(8,128)}) %reduce-scatter.6.cloned.1.call-update) | async-done | bytes 1048592 | tf_op jit(solution)/shard_map/reduce_scatter | solution.py:61
  543.1 96.6 %reduce-scatter.8.cloned.1.call-done = f32[64,4096]{1,0:T(8,128)} async-done(((f32[512,4096]{1,0:T(8,128)}), f32[64,4096]{1,0:T(8,128)}) %reduce-scatter.8.cloned.1.call-update) | async-done | bytes 1048592 | tf_op jit(solution)/shard_map/reduce_scatter | solution.py:62
  (36 shorter events, 12.1 us)
Async XLA Ops:
  7.2 159.7 %all-gather.3.cloned.1.call-start = ((), (), s32[]{:S(2)}) async-start(), calls=%async_computation.3 | async-start | bytes 4325376 | tf_op jit(solution)/shard_map/all_gather | solution.py:41
  9.6 64.7 %copy-start.2 = (s32[16]{0:T(128)S(1)}, s32[16]{0:T(128)}, u32[]{:S(2)}) copy-start(s32[16]{0:T(128)} %param.11) | copy-start | bytes 196
  76.4 177.0 %all-gather.5.cloned.1.call-start = ((), (), s32[]{:S(2)}) async-start(), calls=%async_computation.5 | async-start | bytes 4325376 | tf_op jit(solution)/shard_map/all_gather | solution.py:47
  77.2 366.4 %reduce-scatter.4.cloned.1.call-start = ((), (), s32[]{:S(2)}) async-start(), calls=%async_computation.4 | async-start | bytes 8650752 | tf_op jit(solution)/shard_map/reduce_scatter | solution.py:45
  166.9 5.9 copy-start.1
  178.5 364.6 %reduce-scatter.6.cloned.1.call-start = ((), (), s32[]{:S(2)}) async-start(), calls=%async_computation.6 | async-start | bytes 9437184 | tf_op jit(solution)/shard_map/reduce_scatter | solution.py:61
  253.4 6.1 copy-start
  265.3 374.5 %reduce-scatter.8.cloned.1.call-start = ((), (), s32[]{:S(2)}) async-start(), calls=%async_computation.7 | async-start | bytes 9437184 | tf_op jit(solution)/shard_map/reduce_scatter | solution.py:62
Sparse Core Ops, SparseCore 0:
  76.6 90.2 all-gather.2
  168.6 84.7 all-gather.4
  256.0 187.5 reduce-scatter.3
  446.5 96.5 reduce-scatter.5
  546.1 93.5 reduce-scatter.7
where the time goes:
time: 647 us; the launch traced here: 646 us
  waiting for transfers between devices  530 us (82%)
  matrix products  41.2 us (6%)
  other arithmetic  38.8 us (6%)
  loops' own time  15.9 us (2%)
  between operations  13.9 us (2%)
    reduce_scatter x1, waiting for transfers between devices, shards(): lax.psum_scatter(partial_out, ('table', 'tensor'), scatter_dimension=1, t...  170 us
    reduce_scatter x1, waiting for transfers between devices, shards(): lax.psum_scatter(term_in, 'dp', scatter_dimension=0, tiled=True)  97.9 us
    reduce_scatter x1, waiting for transfers between devices, shards(): lax.psum_scatter(term_out, 'dp', scatter_dimension=0, tiled=True)  96.6 us
    all_gather x1, waiting for transfers between devices, shards(): features = lax.all_gather(pooled, ('table', 'tensor'), axis=1, tiled=True)  89.7 us
    all_gather x1, waiting for transfers between devices, shards(): lax.all_gather(cotangent, ('table', 'tensor'), axis=1, tiled=True)  74.9 us
    reduce_sum x8, other arithmetic, add_block(): jnp.sum(masked[:, :, None] == local_ids[None, None, :], axis=1)  29 us
    another operation x1, loops' own time, pool_local(): lax.scan(add_block, jnp.zeros((samples, half_width), jnp.float32), starts)  15.9 us
  transfers between devices with their start and end apart: 5, of which 5 were waited for; matrix products, arithmetic and copies ran while one was open for 5% of the time, Pallas kernels for 0%

commit v1 on v0

v1 whole, which is shorter than its diff:
```python
import functools

import jax
import jax.numpy as jnp
from jax import lax
from jax.experimental import pallas as pl
from jax.experimental.pallas import tpu as pltpu
from jax.sharding import PartitionSpec as P

MESH = pl.DeviceIdType.MESH
F32, BF16 = jnp.float32, jnp.bfloat16
SIDE = 4
DEPTH = 8
LANES = 128
TILE = 512
VOCAB_STEP = 256


def mul128(i):
    return pl.multiple_of(i * LANES, LANES)


def kernel(
    widths, ids, lens, table_hbm, w_in_hbm, w_out_hbm, cot_hbm,
    mixed, grad_in, grad_out,
    table, w_in, w_out, cot, feat, wide, counts, pooled, gh, pre, hid, hid_t, gp,
    part, pair, st1, st2, row_sum, z_in, z_out,
    in_sem, ag_send, ag_recv, rs_send, rs_recv, z_send, z_recv,
):
    t, yh, z = lax.axis_index("table"), lax.axis_index("tensor"), lax.axis_index("dp")
    core = lax.rem(t, 2)
    x = lax.rem(lax.div(t, 2), SIDE)
    y = yh * 2 + lax.div(t, 2 * SIDE)
    turn = 1 - 2 * core
    samples, bag = ids.shape
    half = samples // 2

    def ring(i):
        return lax.rem(i + 2 * SIDE, SIDE)

    def ring_z(i):
        return lax.rem(i + 2 * DEPTH, DEPTH)

    def dev(px, py, c, pz):
        return {"table": (lax.rem(py, 2) * SIDE + px) * 2 + c, "tensor": lax.div(py, 2), "dp": pz}

    def block(px, py, c):
        return ((lax.rem(py, 2) * SIDE + px) * 2 + c) * 2 + lax.div(py, 2)

    def place(h, a, b):
        return (a, b) if h == 0 else (b, a)

    first = (x, y)
    second = (y, x)

    def peer(h, a, b):
        px, py = place(h, a, b)
        return dev(px, py, core, z)

    partner = dev(x, y, 1 - core, z)

    loads = [
        pltpu.make_async_copy(cot_hbm, cot.at[:, pl.ds(mul128(block(x, y, core)), LANES)], in_sem.at[0]),
        pltpu.make_async_copy(table_hbm, table, in_sem.at[1]),
        pltpu.make_async_copy(w_out_hbm, w_out, in_sem.at[2]),
        pltpu.make_async_copy(w_in_hbm, w_in, in_sem.at[3]),
    ]
    for load in loads:
        load.start()

    barrier = pltpu.get_barrier_semaphore()
    neighbours = [
        dev(ring(x + 1), y, core, z), dev(ring(x - 1), y, core, z),
        dev(x, ring(y + 1), core, z), dev(x, ring(y - 1), core, z),
        dev(x, y, core, ring_z(z + 1)), dev(x, y, core, ring_z(z - 1)), partner,
    ]
    for neighbour in neighbours:
        pl.semaphore_signal(barrier, inc=1, device_id=neighbour, device_id_type=MESH)
    pl.semaphore_wait(barrier, len(neighbours))

    def remote(src, dst, s, r, to):
        return pltpu.make_async_remote_copy(
            src_ref=src, dst_ref=dst, send_sem=s, recv_sem=r, device_id=to, device_id_type=MESH
        )

    sends = []

    def gather(which, buf):
        def view(h, a, b, c):
            px, py = place(h, a, b)
            return buf.at[pl.ds(h * half, half), pl.ds(mul128(block(px, py, c)), LANES)]

        def base(h):
            return (which * 2 + h) * 31

        def copy(h, a, b, slot, recv_slot, to):
            ref = view(h, a, b, core)
            c = remote(ref, ref, ag_send.at[base(h) + slot], ag_recv.at[base(h) + recv_slot], to)
            c.start()
            sends.append(c)

        def arrived(h, a, b, recv_slot, c):
            ref = view(h, a, b, c)
            remote(ref, ref, ag_send.at[base(h)], ag_recv.at[base(h) + recv_slot], partner).wait_recv()

        def to_partner(h, a, b, n):
            copy(h, a, b, 15 + n, 15 + n, partner)

        def offset(j):
            return (0, -turn, turn, 2)[j]

        def line(h, j):
            a, b = first[h], second[h]
            aj = ring(a + offset(j))
            copy(h, aj, b, 3 + 3 * j, 3 + 3 * j + core, peer(h, a, ring(b + turn)))
            copy(h, aj, b, 4 + 3 * j, 3 + 3 * j + (1 - core), peer(h, a, ring(b - turn)))

        def begin():
            for h in range(2):
                a, b = first[h], second[h]
                copy(h, a, b, 0, core, peer(h, ring(a + turn), b))
                copy(h, a, b, 1, 1 - core, peer(h, ring(a - turn), b))
            for h in range(2):
                line(h, 0)
                to_partner(h, first[h], second[h], 0)

        def near(h):
            a, b = first[h], second[h]
            aj = ring(a - turn)
            arrived(h, aj, b, core, core)
            copy(h, aj, b, 2, 2, peer(h, ring(a + turn), b))
            line(h, 1)
            to_partner(h, aj, b, 1)

        def other(h):
            a, b = first[h], second[h]
            aj = ring(a + turn)
            arrived(h, aj, b, 1 - core, core)
            line(h, 2)
            to_partner(h, aj, b, 2)

        def far(h):
            a, b = first[h], second[h]
            aj = ring(a + 2)
            arrived(h, aj, b, 2, core)
            line(h, 3)
            to_partner(h, aj, b, 3)

        def cross(h, j):
            a, b = first[h], second[h]
            aj = ring(a + offset(j))
            bj = ring(b - turn)
            arrived(h, aj, bj, 3 + 3 * j + core, core)
            copy(h, aj, bj, 5 + 3 * j, 5 + 3 * j, peer(h, a, ring(b + turn)))
            to_partner(h, aj, bj, 4 + 3 * j)
            bj = ring(b + turn)
            arrived(h, aj, bj, 3 + 3 * j + (1 - core), core)
            to_partner(h, aj, bj, 5 + 3 * j)

        def cross_far(h, j):
            a, b = first[h], second[h]
            aj, bj = ring(a + offset(j)), ring(b + 2)
            arrived(h, aj, bj, 5 + 3 * j, core)
            to_partner(h, aj, bj, 6 + 3 * j)

        def partner_in(h):
            a, b = first[h], second[h]
            for n in range(16):
                if n < 4:
                    aj, bj = ring(a + (0, turn, -turn, 2)[n]), b
                else:
                    j, k = divmod(n - 4, 3)
                    aj = ring(a + (0, turn, -turn, 2)[j])
                    bj = ring(b + (turn, -turn, 2)[k])
                arrived(h, aj, bj, 15 + n, 1 - core)

        steps = [
            lambda: (near(0), near(1)),
            lambda: (other(0), other(1)),
            lambda: (far(0), far(1)),
            lambda: (cross(0, 0), cross(1, 0)),
            lambda: (cross(0, 1), cross(1, 1)),
            lambda: (cross(0, 2), cross(1, 2)),
            lambda: (cross(0, 3), cross(1, 3)),
            lambda: [cross_far(h, j) for j in range(4) for h in range(2)],
            lambda: (partner_in(0), partner_in(1)),
        ]
        return begin, steps

    def spread():
        inside = lax.broadcasted_iota(jnp.int32, (samples, bag), 1) < lens[...]
        masked = jnp.where(inside, ids[...], -1)
        for b in range(bag):
            wide[b] = jnp.broadcast_to(masked[:, b : b + 1], (samples, LANES)).astype(jnp.int16)

    def pool(low, high):
        rows = 64

        @pl.loop(low, high)
        def _(v):
            start = v * VOCAB_STEP
            for piece in range(VOCAB_STEP // LANES):
                target = (
                    lax.broadcasted_iota(jnp.int32, (rows, LANES), 1) + (start + piece * LANES)
                ).astype(jnp.int16)
                for r in range(0, samples, rows):
                    total = jnp.zeros((rows, LANES), BF16)
                    for b in range(bag):
                        hit = wide[b, r : r + rows, :] == target
                        total = total + jnp.where(hit, jnp.ones((), BF16), jnp.zeros((), BF16))
                    counts[r : r + rows, piece * LANES : (piece + 1) * LANES] = total
            picked = table[pl.ds(pl.multiple_of(start, VOCAB_STEP), VOCAB_STEP), :]
            pooled[...] += jnp.dot(counts[...], picked, preferred_element_type=F32)

    def pool_end():
        mean = pooled[...] / lens[...].astype(F32)
        column = lax.broadcasted_iota(jnp.int32, (samples, LANES), 1) + yh * LANES
        mean = jnp.where(column < widths[t], mean, jnp.zeros_like(mean))
        feat[:, pl.ds(mul128(block(x, y, core)), LANES)] = mean.astype(BF16)

    def grad_hidden(low, high):
        @pl.loop(low, high)
        def _(k):
            cols = pl.ds(pl.multiple_of(k * TILE, TILE), TILE)
            gh[...] += lax.dot_general(
                cot[:, cols], w_out[:, cols], (((1,), (1,)), ((), ())), preferred_element_type=F32
            )

    def preact():
        @pl.loop(0, feat.shape[1] // TILE)
        def _(k):
            cols = pl.ds(pl.multiple_of(k * TILE, TILE), TILE)
            pre[...] += jnp.dot(feat[:, cols], w_in[cols, :], preferred_element_type=F32)

    begin_cot, cot_steps = gather(0, cot)
    begin_feat, feat_steps = gather(1, feat)
    loads[0].wait()
    begin_cot()
    spread()
    pooled[...] = jnp.zeros_like(pooled)
    gh[...] = jnp.zeros_like(gh)
    pre[...] = jnp.zeros_like(pre)
    loads[1].wait()
    blocks = table.shape[0] // VOCAB_STEP
    quarter = blocks // 4
    for q in range(4):
        pool(q * quarter, (q + 1) * quarter)
        if q < 3:
            cot_steps[q]()
    pool_end()
    begin_feat()
    cot_steps[3]()
    cot_steps[4]()
    feat_steps[0]()
    cot_steps[5]()
    feat_steps[1]()
    cot_steps[6]()
    feat_steps[2]()
    cot_steps[7]()
    feat_steps[3]()
    cot_steps[8]()
    loads[2].wait()
    tiles = cot.shape[1] // TILE
    for q in range(4):
        grad_hidden(q * tiles // 4, (q + 1) * tiles // 4)
        feat_steps[4 + q]()
    loads[3].wait()
    feat_steps[8]()
    preact()

    rows = 64

    @pl.loop(0, samples // rows)
    def _(i):
        r = pl.ds(pl.multiple_of(i * rows, rows), rows)
        value = pre[r, :]
        gate = jax.nn.sigmoid(value)
        hid[r, :] = (value * gate).astype(BF16)
        gp[r, :] = (gh[r, :] * (gate * (1.0 + value * (1.0 - gate)))).astype(BF16)

    hid_t[...] = jnp.transpose(hid[...])

    in_rows, in_cols = grad_in.shape
    out_rows, out_cols = grad_out.shape

    def add_in(d, terms, store):
        step = 128

        @pl.loop(0, in_rows // step)
        def _(i):
            r = pl.ds(pl.multiple_of(i * step, step), step)
            cols = pl.ds(pl.multiple_of(d * in_rows + i * step, step), step)
            own = lax.dot_general(feat[:, cols], gp[...], (((0,), (0,)), ((), ())), preferred_element_type=F32)
            for term in terms:
                own = own + term[r, :].astype(F32)
            store[r, :] = own.astype(store.dtype)

    def add_out(d, terms, store):
        @pl.loop(0, out_cols // TILE)
        def _(j):
            cols = pl.ds(pl.multiple_of(j * TILE, TILE), TILE)
            lhs = hid_t[pl.ds(pl.multiple_of(d * out_rows, out_rows), out_rows), :]
            own = jnp.dot(lhs, cot[:, cols], preferred_element_type=F32)
            for term in terms:
                own = own + term[:, cols].astype(F32)
            store[:, cols] = own.astype(store.dtype)

    up, down = dev(x, y, core, ring_z(z + 1)), dev(x, y, core, ring_z(z - 1))
    chains = {"in+": (0, 4, 1), "in-": (4, 3, -1), "out+": (0, 3, 1), "out-": (3, 4, -1)}

    def z_copy(name, s):
        slot, hops, sign = chains[name]
        slots, starts = (z_in, 0) if name[:2] == "in" else (z_out, 7)
        first_slot = 7 + (0 if sign > 0 else 1)
        src = slots.at[first_slot] if s == 0 else slots.at[slot + s - 1]
        sem = starts + slot + s
        return remote(src, slots.at[slot + s], z_send.at[sem], z_recv.at[sem], up if sign > 0 else down)

    def z_step(name, s):
        slot, hops, sign = chains[name]
        slots = z_in if name[:2] == "in" else z_out
        add = add_in if name[:2] == "in" else add_out
        d = ring_z(z + sign * (hops - s))
        if s == 0:
            add(d, [], slots.at[7 + (0 if sign > 0 else 1)])
        else:
            z_copy(name, s - 1).wait_recv()
            add(d, [slots.at[slot + s - 1]], slots.at[slot + s - 1])
        c = z_copy(name, s)
        c.start()
        sends.append(c)

    def rs(h, n, src, dst, to):
        i = h * 15 + n
        c = remote(src, dst, rs_send.at[i], rs_recv.at[i], to)
        c.start()
        sends.append(c)

    def rs_wait(h, n, ref):
        i = h * 15 + n
        remote(ref, ref, rs_send.at[i], rs_recv.at[i], partner).wait_recv()

    def cols_of(px, py, c):
        return pl.ds(mul128(block(px, py, c)), LANES)

    def out_partial():
        @pl.loop(0, part.shape[1] // TILE)
        def _(j):
            cols = pl.ds(pl.multiple_of(j * TILE, TILE), TILE)
            part[:, cols] = jnp.dot(hid[...], w_out[:, cols], preferred_element_type=F32).astype(BF16)

    def pair_copy(n):
        px, py = divmod(n, SIDE)
        return remote(
            part.at[:, cols_of(px, py, 1 - core)], pair.at[n], rs_send.at[30 + n], rs_recv.at[30 + n], partner
        )

    def pair_send():
        for n in range(SIDE * SIDE):
            c = pair_copy(n)
            c.start()
            sends.append(c)

    def pair_add():
        for n in range(SIDE * SIDE):
            pair_copy(n).wait_recv()

        @pl.loop(0, SIDE * SIDE)
        def _(n):
            px, py = lax.div(n, SIDE), lax.rem(n, SIDE)
            both = part[:, cols_of(px, py, core)].astype(F32) + pair[n].astype(F32)
            pair[n] = both.astype(BF16)

    def chip(h, a, b):
        px, py = (b, a) if h == 0 else (a, b)
        return pair.at[px * SIDE + py, pl.ds(h * half, half), :]

    def along(h, da, db):
        if h == 0:
            return dev(ring(x + db), ring(y + da), core, z)
        return dev(ring(x + da), ring(y + db), core, z)

    def axes(h):
        return (y, x) if h == 0 else (x, y)

    def rs_first():
        for h in range(2):
            a, b = axes(h)
            for k in range(SIDE):
                rs(h, k, chip(h, ring(a + 2), k), st1.at[h, 0, k], along(h, turn, 0))
                rs(h, 4 + k, chip(h, ring(a - turn), k), st1.at[h, 1, k], along(h, -turn, 0))

    def rs_second():
        for h in range(2):
            a, b = axes(h)
            for k in range(SIDE):
                rs_wait(h, k, st1.at[h, 0, k])
                own = chip(h, ring(a + turn), k)[...].astype(F32)
                st1[h, 0, k] = (own + st1[h, 0, k].astype(F32)).astype(BF16)
                rs(h, 8 + k, st1.at[h, 0, k], st1.at[h, 2, k], along(h, turn, 0))

    def rs_third():
        for h in range(2):
            a, b = axes(h)
            for k in range(SIDE):
                rs_wait(h, 4 + k, st1.at[h, 1, k])
                rs_wait(h, 8 + k, st1.at[h, 2, k])
                own = chip(h, a, k)[...].astype(F32)
                row_sum[h, k] = own + st1[h, 1, k].astype(F32) + st1[h, 2, k].astype(F32)
            st2[h, 3] = row_sum[h, ring(b + 2)].astype(BF16)
            rs(h, 12, st2.at[h, 3], st2.at[h, 0], along(h, 0, turn))
            st2[h, 4] = row_sum[h, ring(b - turn)].astype(BF16)
            rs(h, 13, st2.at[h, 4], st2.at[h, 1], along(h, 0, -turn))

    def rs_fourth():
        for h in range(2):
            a, b = axes(h)
            rs_wait(h, 12, st2.at[h, 0])
            st2[h, 5] = (row_sum[h, ring(b + turn)] + st2[h, 0].astype(F32)).astype(BF16)
            rs(h, 14, st2.at[h, 5], st2.at[h, 2], along(h, 0, turn))

    def rs_last():
        for h in range(2):
            a, b = axes(h)
            rs_wait(h, 13, st2.at[h, 1])
            rs_wait(h, 14, st2.at[h, 2])
            total = row_sum[h, b] + st2[h, 1].astype(F32) + st2[h, 2].astype(F32)
            mixed[h * half : (h + 1) * half, :] = total.astype(BF16)

    z_step("in+", 0)
    z_step("out-", 0)
    z_step("out+", 0)
    z_step("in-", 0)
    out_partial()
    pair_send()
    pair_add()
    rs_first()
    z_step("in+", 1)
    z_step("out-", 1)
    rs_second()
    z_step("out+", 1)
    z_step("in-", 1)
    rs_third()
    z_step("in+", 2)
    z_step("out-", 2)
    rs_fourth()
    z_step("out+", 2)
    z_step("in-", 2)
    rs_last()
    z_step("in+", 3)
    z_step("out-", 3)
    for name in ("out+", "in-", "in+", "out-"):
        slot, hops, sign = chains[name]
        z_copy(name, hops - 1).wait_recv()
        if name == "in+":
            add_in(z, [z_in.at[3], z_in.at[6]], grad_in)
        if name == "out-":
            add_out(z, [z_out.at[2], z_out.at[6]], grad_out)
    for c in sends:
        c.wait_send()


def shards(lookup_ids, bag_lengths, feature_widths, tables, w_in, w_out, cotangent):
    samples, bag = lookup_ids.shape[0], lookup_ids.shape[2]
    vocab = tables.shape[1]
    wide_in, hidden = w_in.shape
    wide_out = w_out.shape[1]
    in_rows, out_rows = wide_in // DEPTH, hidden // DEPTH
    half = samples // 2
    vmem = pl.BlockSpec(memory_space=pltpu.VMEM)
    hbm = pl.BlockSpec(memory_space=pl.ANY)
    dma = pltpu.SemaphoreType.DMA
    return pl.pallas_call(
        kernel,
        out_shape=(
            jax.ShapeDtypeStruct((samples, LANES), BF16),
            jax.ShapeDtypeStruct((in_rows, hidden), F32),
            jax.ShapeDtypeStruct((out_rows, wide_out), F32),
        ),
        in_specs=[pl.BlockSpec(memory_space=pltpu.SMEM), vmem, vmem, hbm, hbm, hbm, hbm],
        out_specs=(vmem, vmem, vmem),
        scratch_shapes=[
            pltpu.VMEM((vocab, LANES), BF16),
            pltpu.VMEM((wide_in, hidden), BF16),
            pltpu.VMEM((hidden, wide_out), BF16),
            pltpu.VMEM((samples, wide_out), BF16),
            pltpu.VMEM((samples, wide_in), BF16),
            pltpu.VMEM((bag, samples, LANES), jnp.int16),
            pltpu.VMEM((samples, VOCAB_STEP), BF16),
            pltpu.VMEM((samples, LANES), F32),
            pltpu.VMEM((samples, hidden), F32),
            pltpu.VMEM((samples, hidden), F32),
            pltpu.VMEM((samples, hidden), BF16),
            pltpu.VMEM((hidden, samples), BF16),
            pltpu.VMEM((samples, hidden), BF16),
            pltpu.VMEM((samples, wide_out), BF16),
            pltpu.VMEM((SIDE * SIDE, samples, LANES), BF16),
            pltpu.VMEM((2, 3, SIDE, half, LANES), BF16),
            pltpu.VMEM((2, 6, half, LANES), BF16),
            pltpu.VMEM((2, SIDE, half, LANES), F32),
            pltpu.VMEM((9, in_rows, hidden), BF16),
            pltpu.VMEM((9, out_rows, wide_out), BF16),
            dma((4,)),
            dma((124,)),
            dma((124,)),
            dma((46,)),
            dma((46,)),
            dma((14,)),
            dma((14,)),
        ],
        compiler_params=pltpu.CompilerParams(
            collective_id=0, has_side_effects=True, vmem_limit_bytes=63 * 1024 * 1024
        ),
    )(feature_widths, lookup_ids[:, 0, :], bag_lengths, tables[0], w_in, w_out, cotangent)


def solution(mesh):
    return jax.shard_map(
        shards,
        mesh=mesh,
        in_specs=(
            P("dp", "table", None),
            P("dp", "table"),
            P(),
            P("table", None, "tensor"),
            P(None, ("table", "tensor")),
            P(("table", "tensor"), None),
            P("dp", ("table", "tensor")),
        ),
        out_specs=(
            P("dp", ("table", "tensor")),
            P("dp", ("table", "tensor")),
            P(("table", "tensor", "dp"), None),
        ),
        check_vma=False,
    )
```

time: 647 us -> 152 us (0.23)
  waiting for transfers between devices: 530 us -> 0 us
  Pallas kernels: 0 us -> 142 us
  matrix products: 41.2 us -> 0 us
  other arithmetic: 38.8 us -> 0 us
  loops' own time: 15.9 us -> 0 us
  between operations: 13.9 us -> 0.64 us
    reduce_scatter x3 -> x0, waiting for transfers between devices: 365 us -> none  [the longest x1 170 us: shards(): lax.psum_scatter(partial_out, ('table', 'tensor'), scatter_dimension=1, t...]
    all_gather x2 -> x0, waiting for transfers between devices: 165 us -> none  [the longest x1 89.7 us: shards(): features = lax.all_gather(pooled, ('table', 'tensor'), axis=1, tiled=True)]
    pallas_call x0 -> x1, Pallas kernels: none -> 142 us  [shards(): pl.pallas_call(kernel, out_shape=(jax.ShapeDtypeStruct((samples, LANES),...]
    dot_general x13 -> x0, matrix products: 41.2 us -> none  [the longest x8 9.94 us: add_block(): jnp.dot(counts, table_rows, preferred_element_type=jnp.float32)]
    reduce_sum x8 -> x0, other arithmetic: 29 us -> none  [add_block(): jnp.sum(masked[:, :, None] == local_ids[None, None, :], axis=1)]
    another operation x1 -> x0, loops' own time: 15.9 us -> none  [pool_local(): lax.scan(add_block, jnp.zeros((samples, half_width), jnp.float32), starts)]
    unnamed x7 -> x5, local copies, waits for them, and re-layouts: 0.89 us -> 9.23 us
  transfers between devices with their start and end apart: 5 -> 0, of which waited for: 5 -> 0; matrix products, arithmetic and copies ran while one was open for 5% -> 0% of each run, Pallas kernels for 0% -> 0%
where the time goes in v1:
time: 152 us; the launch traced here: 151 us
  Pallas kernels  142 us (93%)
  local copies, waits for them, and re-layouts  9.23 us (6%)
    pallas_call x1, Pallas kernels, shards(): pl.pallas_call(kernel, out_shape=(jax.ShapeDtypeStruct((samples, LANES),...  142 us
    unnamed x5, local copies, waits for them, and re-layouts  9.23 us

profile of v1, /device:TPU:1, one launch (start us, length us, event | category | flops | bytes accessed | tf_op | source)
XLA Modules:
  0.0 151.4 jit_solution(8237027716967034229)
XLA Ops:
  0.6 1.6 %copy.10 = s32[512,1,16]{2,0,1:T(8,128)} copy(s32[512,1,16]{0,2,1:T(8,128)} %param.7) | data formatting | bytes 65536 | tf_op args[0]
  2.2 1.5 %copy.11.lens = s32[512,1]{1,0:T(8,128)} copy(s32[512,1]{0,1:T(1,128)} %param.8) | data formatting | bytes 4096 | tf_op args[1]
  3.8 141.5 %shard_map.94 = (bf16[512,128]{1,0:T(8,128)(2,1)}, f32[512,512]{1,0:T(8,128)}, f32[64,4096]{1,0:T(8,128)}) custom-call(s32[16]{0:T(128)} %widths.1, s32[512,16]{1,0:T(8,128)} %bitcast.3, s32[512,1]{1,0:T(8,128)} %copy.11.lens, bf16[4096,128]{1,0:T(8,128)(2,1)} %bitcast.2, bf16[4096,512]{1,0:T(8,128)(2,1)} %w_in_hbm.1, bf16[512,4096]{1,0:T(8,128)(2,1)} %w_out_hbm.1, ...), custom_call_target="tpu_custom_call" | custom-call | tf_op jit(solution)/shard_map/pallas_call | solution.py:473
  145.3 1.6 %copy.15 = bf16[512,128]{1,0:T(8,128)(2,1)} copy(bf16[512,128]{1,0:T(8,128)(2,1)} %get-tuple-element.6) | data formatting | bytes 262144
  146.9 2.3 %copy.16 = f32[512,512]{1,0:T(8,128)} copy(f32[512,512]{1,0:T(8,128)} %get-tuple-element.7) | data formatting | bytes 2097152
  149.1 2.3 %copy.17 = f32[64,4096]{1,0:T(8,128)} copy(f32[64,4096]{1,0:T(8,128)} %get-tuple-element.8) | data formatting | bytes 2097152

commit v2 on v1

v2 whole, which is shorter than its diff:
```python
import functools

import jax
import jax.numpy as jnp
from jax import lax
from jax.experimental import pallas as pl
from jax.experimental.pallas import tpu as pltpu
from jax.sharding import PartitionSpec as P

MESH = pl.DeviceIdType.MESH
F32, BF16 = jnp.float32, jnp.bfloat16
SIDE = 4
DEPTH = 8
LANES = 128
TILE = 512
PLAN_BEFORE = ((), (), (), (0, 1), (), (2,), (3,), ())
PLAN_AFTER = ((0, 4), (1, 0), (0, 5), (1, 1), (0, 6), (1, 2), (1, 3), (0, 7), (1, 4), (1, 5), (1, 6), (0, 8), (1, 7))
PIECES = 8
FIELDS = 4


def mul128(i):
    return pl.multiple_of(i * LANES, LANES)


def kernel(
    widths, ids, lens, table_hbm, w_in_hbm, w_out_hbm, cot_hbm,
    mixed, grad_in, grad_out,
    table, w_in, w_out, cot, feat, keys, spans, counts, gh, pre, hid, hid_t, gp,
    part, pair, st1, st2, row_sum, z_in, z_out,
    in_sem, ag_send, ag_recv, rs_send, rs_recv, z_send, z_recv,
):
    t, yh, z = lax.axis_index("table"), lax.axis_index("tensor"), lax.axis_index("dp")
    core = lax.rem(t, 2)
    x = lax.rem(lax.div(t, 2), SIDE)
    y = yh * 2 + lax.div(t, 2 * SIDE)
    turn = 1 - 2 * core
    bag, samples = ids.shape
    half = samples // 2

    def ring(i):
        return lax.rem(i + 2 * SIDE, SIDE)

    def ring_z(i):
        return lax.rem(i + 2 * DEPTH, DEPTH)

    def dev(px, py, c, pz):
        return {"table": (lax.rem(py, 2) * SIDE + px) * 2 + c, "tensor": lax.div(py, 2), "dp": pz}

    def block(px, py, c):
        return ((lax.rem(py, 2) * SIDE + px) * 2 + c) * 2 + lax.div(py, 2)

    def place(h, a, b):
        return (a, b) if h == 0 else (b, a)

    first = (x, y)
    second = (y, x)

    def peer(h, a, b):
        px, py = place(h, a, b)
        return dev(px, py, core, z)

    partner = dev(x, y, 1 - core, z)

    loads = [
        pltpu.make_async_copy(cot_hbm, cot.at[:, pl.ds(mul128(block(x, y, core)), LANES)], in_sem.at[0]),
        pltpu.make_async_copy(table_hbm, table, in_sem.at[1]),
        pltpu.make_async_copy(w_out_hbm, w_out, in_sem.at[2]),
        pltpu.make_async_copy(w_in_hbm, w_in, in_sem.at[3]),
    ]
    for load in loads:
        load.start()

    barrier = pltpu.get_barrier_semaphore()
    neighbours = [
        dev(ring(x + 1), y, core, z), dev(ring(x - 1), y, core, z),
        dev(x, ring(y + 1), core, z), dev(x, ring(y - 1), core, z),
        dev(x, y, core, ring_z(z + 1)), dev(x, y, core, ring_z(z - 1)), partner,
    ]
    for neighbour in neighbours:
        pl.semaphore_signal(barrier, inc=1, device_id=neighbour, device_id_type=MESH)

    def remote(src, dst, s, r, to):
        return pltpu.make_async_remote_copy(
            src_ref=src, dst_ref=dst, send_sem=s, recv_sem=r, device_id=to, device_id_type=MESH
        )

    def gather(which, buf, row, rows):
        def view(h, a, b, c):
            px, py = place(h, a, b)
            return buf.at[pl.ds(row + h * (rows // 2), rows // 2), pl.ds(mul128(block(px, py, c)), LANES)]

        def copy(h, a, b, recv_slot, to):
            ref = view(h, a, b, core)
            remote(ref, ref, ag_send.at[which], ag_recv.at[which * 16 + recv_slot], to).start()

        def arrived(recv_slot, blocks=1):
            ref = buf.at[:rows, : blocks * LANES]
            remote(ref, ref, ag_send.at[which], ag_recv.at[which * 16 + recv_slot], partner).wait_recv()

        def sent():
            ref = buf.at[:rows, : 31 * LANES]
            remote(ref, ref, ag_send.at[which], ag_recv.at[which * 16], partner).wait_send()

        def to_partner(h, a, b):
            copy(h, a, b, 15, partner)

        def offset(j):
            return (0, -turn, turn, 2)[j]

        def line(h, j):
            a, b = first[h], second[h]
            aj = ring(a + offset(j))
            copy(h, aj, b, 3 + 3 * j + core, peer(h, a, ring(b + turn)))
            copy(h, aj, b, 3 + 3 * j + (1 - core), peer(h, a, ring(b - turn)))

        def begin():
            for h in range(2):
                a, b = first[h], second[h]
                copy(h, a, b, core, peer(h, ring(a + turn), b))
                copy(h, a, b, 1 - core, peer(h, ring(a - turn), b))
            for h in range(2):
                line(h, 0)
                to_partner(h, first[h], second[h])

        def near():
            arrived(core)
            for h in range(2):
                a, b = first[h], second[h]
                aj = ring(a - turn)
                copy(h, aj, b, 2, peer(h, ring(a + turn), b))
                line(h, 1)
                to_partner(h, aj, b)

        def other():
            arrived(1 - core)
            for h in range(2):
                line(h, 2)
                to_partner(h, ring(first[h] + turn), second[h])

        def far():
            arrived(2)
            for h in range(2):
                line(h, 3)
                to_partner(h, ring(first[h] + 2), second[h])

        def cross(j):
            arrived(3 + 3 * j + core)
            for h in range(2):
                a, b = first[h], second[h]
                aj, bj = ring(a + offset(j)), ring(b - turn)
                copy(h, aj, bj, 5 + 3 * j, peer(h, a, ring(b + turn)))
                to_partner(h, aj, bj)
            arrived(3 + 3 * j + (1 - core))
            for h in range(2):
                to_partner(h, ring(first[h] + offset(j)), ring(second[h] + turn))

        def cross_far(j):
            arrived(5 + 3 * j)
            for h in range(2):
                to_partner(h, ring(first[h] + offset(j)), ring(second[h] + 2))

        steps = [
            near,
            other,
            far,
            lambda: cross(0),
            lambda: cross(1),
            lambda: cross(2),
            lambda: cross(3),
            lambda: [cross_far(j) for j in range(4)],
            lambda: arrived(15, 16),
        ]
        return begin, steps, sent

    vocab = table.shape[0]
    words = vocab // FIELDS

    def spread():
        inside = lax.broadcasted_iota(jnp.int32, (bag, samples), 0) < lens[...]
        field = lax.shift_right_logical(ids[...], words.bit_length() - 1)
        code = lax.bitwise_and(ids[...], words - 1) + field * (8 << 16)
        keys[...] = jnp.transpose(jnp.where(inside, code, 2 * words))

        spans[...] = jnp.transpose(jnp.broadcast_to(lens[...], (8, samples)).astype(F32))

    piece = counts.shape[1]

    def count(n):
        rows = 8
        lane = lax.broadcasted_iota(jnp.int32, (rows, LANES), 1)
        for g in range(0, piece, rows):
            code = keys[n * piece + g : n * piece + g + rows, :]
            spread_keys, spread_units = [], []
            for b in range(bag):
                wide = jnp.broadcast_to(code[:, b : b + 1], (rows, LANES))
                spread_keys.append(lax.bitwise_and(wide, 0xFFFF))
                spread_units.append(lax.shift_left(jnp.ones_like(wide), lax.shift_right_logical(wide, 16)))
            for w in range(0, words, LANES):
                target = lane + w
                parts = []
                for b in range(bag):
                    parts.append(jnp.where(spread_keys[b] == target, spread_units[b], 0))
                while len(parts) > 1:
                    parts = [p + q for p, q in zip(parts[::2], parts[1::2])]
                for f in range(FIELDS):
                    number = lax.bitwise_and(lax.shift_right_logical(parts[0], 8 * f), 255)
                    at = f * words + w
                    counts[n % 2, g : g + rows, at : at + LANES] = number.astype(F32).astype(BF16)

    def pool_end(n):
        r = slice(n * piece, (n + 1) * piece)
        summed = jnp.dot(counts[n % 2], table[...], preferred_element_type=F32)
        mean = summed / spans[r, 0:1]
        column = lax.broadcasted_iota(jnp.int32, (piece, LANES), 1) + yh * LANES
        mean = jnp.where(column < widths[t], mean, jnp.zeros_like(mean))
        feat[r, pl.ds(mul128(block(x, y, core)), LANES)] = mean.astype(BF16)

    def grad_hidden(low, high):
        @pl.loop(low, high)
        def _(k):
            cols = pl.ds(pl.multiple_of(k * TILE, TILE), TILE)
            gh[...] += lax.dot_general(
                cot[:, cols], w_out[:, cols], (((1,), (1,)), ((), ())), preferred_element_type=F32
            )

    def preact(parity):
        width = 4 * LANES // 2

        @pl.loop(0, feat.shape[1] // (2 * width))
        def _(k):
            cols = pl.ds(pl.multiple_of((2 * k + parity) * width, width), width)
            pre[...] += jnp.dot(feat[:, cols], w_in[cols, :], preferred_element_type=F32)

    begin_cot, cot_steps, cot_sent = gather(0, cot, 0, samples)
    begin_feat, feat_steps, feat_sent = gather(1, feat, 0, samples)
    tiles = cot.shape[1] // TILE
    spread()
    gh[...] = jnp.zeros_like(gh)
    pre[...] = jnp.zeros_like(pre)
    for n in range(PIECES):
        count(n)
        if n == 0:
            loads[1].wait()
            pl.semaphore_wait(barrier, len(neighbours))
            loads[0].wait()
            begin_cot()
        else:
            pool_end(n - 1)
        for k in PLAN_BEFORE[n]:
            cot_steps[k]()
    pool_end(PIECES - 1)
    begin_feat()
    loads[2].wait()
    for which, n in PLAN_AFTER:
        (cot_steps, feat_steps)[which][n]()
    loads[3].wait()
    preact(core)
    feat_steps[8]()
    preact(1 - core)

    rows = 64

    @pl.loop(0, samples // rows)
    def _(i):
        r = pl.ds(pl.multiple_of(i * rows, rows), rows)
        value = pre[r, :]
        gate = jax.nn.sigmoid(value)
        hid[r, :] = (value * gate).astype(BF16)
        pre[r, :] = gate * (1.0 + value * (1.0 - gate))

    hid_t[...] = jnp.transpose(hid[...])

    def grad_preact():
        grad_hidden(0, tiles)

        @pl.loop(0, samples // rows)
        def _(i):
            r = pl.ds(pl.multiple_of(i * rows, rows), rows)
            gp[r, :] = (gh[r, :] * pre[r, :]).astype(BF16)

    in_rows, in_cols = grad_in.shape
    out_rows, out_cols = grad_out.shape

    def add_in(d, terms, store, low, high):
        step = 128

        @pl.loop(low // step, high // step)
        def _(i):
            r = pl.ds(pl.multiple_of(i * step, step), step)
            cols = pl.ds(pl.multiple_of(d * in_rows + i * step, step), step)
            own = lax.dot_general(feat[:, cols], gp[...], (((0,), (0,)), ((), ())), preferred_element_type=F32)
            for term in terms:
                own = own + term[r, :].astype(F32)
            store[r, :] = own.astype(store.dtype)

    def add_out(d, terms, store):
        @pl.loop(0, out_cols // TILE)
        def _(j):
            cols = pl.ds(pl.multiple_of(j * TILE, TILE), TILE)
            lhs = hid_t[pl.ds(pl.multiple_of(d * out_rows, out_rows), out_rows), :]
            own = jnp.dot(lhs, cot[:, cols], preferred_element_type=F32)
            for term in terms:
                own = own + term[:, cols].astype(F32)
            store[:, cols] = own.astype(store.dtype)

    up, down = dev(x, y, core, ring_z(z + 1)), dev(x, y, core, ring_z(z - 1))
    chains = {"out+": (0, 4, 1), "out-": (4, 3, -1), "in+": (0, 3, 1), "in-": (3, 4, -1)}
    in_half = in_rows // 2

    def start_slot(name):
        return 7 + (0 if name.endswith("+") else 1)

    def z_copy(name, s, n=0):
        slot, hops, sign = chains[name]
        from_slot = start_slot(name) if s == 0 else slot + s - 1
        to = up if sign > 0 else down
        if name[:3] == "out":
            return remote(z_out.at[from_slot], z_out.at[slot + s], z_send.at[1], z_recv.at[14 + slot + s], to)
        r = pl.ds(n * in_half, in_half)
        return remote(z_in.at[from_slot, r], z_in.at[slot + s, r], z_send.at[0], z_recv.at[n * 7 + slot + s], to)

    def z_step(name, s):
        slot, hops, sign = chains[name]
        d = ring_z(z + sign * (hops - s))
        for n in range(1 if name[:3] == "out" else 2):
            if s > 0:
                z_copy(name, s - 1, n).wait_recv()
            from_slot = start_slot(name) if s == 0 else slot + s - 1
            slots = z_out if name[:3] == "out" else z_in
            terms = [slots.at[from_slot]] if s > 0 else []
            if name[:3] == "out":
                add_out(d, terms, slots.at[from_slot])
            else:
                add_in(d, terms, slots.at[from_slot], n * in_half, (n + 1) * in_half)
            z_copy(name, s, n).start()

    def rs(h, n, src, dst, to):
        remote(src, dst, rs_send.at[0], rs_recv.at[h * 6 + n], to).start()

    def rs_wait(h, n, ref):
        remote(ref, ref, rs_send.at[0], rs_recv.at[h * 6 + n], partner).wait_recv()

    def cols_of(px, py, c):
        return pl.ds(mul128(block(px, py, c)), LANES)

    def out_partial():
        @pl.loop(0, part.shape[1] // TILE)
        def _(j):
            cols = pl.ds(pl.multiple_of(j * TILE, TILE), TILE)
            part[:, cols] = jnp.dot(hid[...], w_out[:, cols], preferred_element_type=F32).astype(BF16)

    def pair_send():
        for n in range(SIDE * SIDE):
            px, py = divmod(n, SIDE)
            remote(part.at[:, cols_of(px, py, 1 - core)], pair.at[n], rs_send.at[1], rs_recv.at[12], partner).start()

    def pair_add():
        remote(pair, pair, rs_send.at[1], rs_recv.at[12], partner).wait_recv()

        @pl.loop(0, SIDE * SIDE)
        def _(n):
            px, py = lax.div(n, SIDE), lax.rem(n, SIDE)
            both = part[:, cols_of(px, py, core)].astype(F32) + pair[n].astype(F32)
            pair[n] = both.astype(BF16)

    def chip(h, a, b):
        px, py = (b, a) if h == 0 else (a, b)
        return pair.at[px * SIDE + py, pl.ds(h * half, half), :]

    def along(h, da, db):
        if h == 0:
            return dev(ring(x + db), ring(y + da), core, z)
        return dev(ring(x + da), ring(y + db), core, z)

    def axes(h):
        return (y, x) if h == 0 else (x, y)

    def rs_first():
        for h in range(2):
            a, b = axes(h)
            for k in range(SIDE):
                rs(h, 0, chip(h, ring(a + 2), k), st1.at[h, 0, k], along(h, turn, 0))
                rs(h, 1, chip(h, ring(a - turn), k), st1.at[h, 1, k], along(h, -turn, 0))

    def rs_second():
        for h in range(2):
            a, b = axes(h)
            rs_wait(h, 0, st1.at[h, 0])
            for k in range(SIDE):
                own = chip(h, ring(a + turn), k)[...].astype(F32)
                st1[h, 0, k] = (own + st1[h, 0, k].astype(F32)).astype(BF16)
                rs(h, 2, st1.at[h, 0, k], st1.at[h, 2, k], along(h, turn, 0))

    def rs_third():
        for h in range(2):
            a, b = axes(h)
            rs_wait(h, 1, st1.at[h, 1])
            rs_wait(h, 2, st1.at[h, 2])
            for k in range(SIDE):
                own = chip(h, a, k)[...].astype(F32)
                row_sum[h, k] = own + st1[h, 1, k].astype(F32) + st1[h, 2, k].astype(F32)
            st2[h, 3] = row_sum[h, ring(b + 2)]
            rs(h, 3, st2.at[h, 3], st2.at[h, 0], along(h, 0, turn))
            st2[h, 4] = row_sum[h, ring(b - turn)]
            rs(h, 4, st2.at[h, 4], st2.at[h, 1], along(h, 0, -turn))

    def rs_fourth():
        for h in range(2):
            a, b = axes(h)
            rs_wait(h, 3, st2.at[h, 0])
            st2[h, 5] = row_sum[h, ring(b + turn)] + st2[h, 0]
            rs(h, 5, st2.at[h, 5], st2.at[h, 2], along(h, 0, turn))

    def rs_last():
        for h in range(2):
            a, b = axes(h)
            rs_wait(h, 4, st2.at[h, 1])
            rs_wait(h, 5, st2.at[h, 2])
            total = row_sum[h, b] + st2[h, 1] + st2[h, 2]
            mixed[h * half : (h + 1) * half, :] = total.astype(BF16)

    z_step("out+", 0)
    z_step("out-", 0)
    grad_preact()
    z_step("in+", 0)
    z_step("in-", 0)
    out_partial()
    pair_send()
    pair_add()
    rs_first()
    z_step("out+", 1)
    z_step("out-", 1)
    rs_second()
    z_step("in+", 1)
    z_step("in-", 1)
    rs_third()
    z_step("out+", 2)
    z_step("out-", 2)
    rs_fourth()
    z_step("in+", 2)
    z_step("in-", 2)
    rs_last()
    z_step("out+", 3)
    z_step("in-", 3)
    add_in(z, [], grad_in, 0, in_rows)
    add_out(z, [], grad_out)
    z_copy("out-", 2).wait_recv()
    grad_out[...] += z_out[6].astype(F32)
    for n in range(2):
        z_copy("in+", 2, n).wait_recv()
    grad_in[...] += z_in[2].astype(F32)
    for n in range(2):
        r = slice(n * in_half, (n + 1) * in_half)
        z_copy("in-", 3, n).wait_recv()
        grad_in[r, :] += z_in[6, r].astype(F32)
    z_copy("out+", 3).wait_recv()
    grad_out[...] += z_out[3].astype(F32)
    cot_sent()
    feat_sent()
    remote(part.at[:, : 18 * LANES], part.at[:, : 18 * LANES], rs_send.at[0], rs_recv.at[0], partner).wait_send()
    remote(pair, pair, rs_send.at[1], rs_recv.at[12], partner).wait_send()
    for i, slots in enumerate((z_in, z_out)):
        remote(slots.at[0:7], slots.at[0:7], z_send.at[i], z_recv.at[7 * i], up).wait_send()


def hand_over_kernel(*refs):
    n = (len(refs) - 2) // 3
    ins, outs, held = refs[:n], refs[n : 2 * n], refs[2 * n : 3 * n]
    sem_in, sem_out = refs[3 * n], refs[3 * n + 1]
    pieces = 2
    reads, writes = [], []
    for k in range(n):
        rows = ins[k].shape[0] // pieces
        for p in range(pieces):
            r = pl.ds(p * rows, rows)
            i = k * pieces + p
            reads.append(pltpu.make_async_copy(ins[k].at[r], held[k].at[r], sem_in.at[i]))
            writes.append(pltpu.make_async_copy(held[k].at[r], outs[k].at[r], sem_out.at[i]))
    for c in reads:
        c.start()
    for c, w in zip(reads, writes):
        c.wait()
        w.start()
    for w in writes:
        w.wait()


def hand_over(arrays):
    hbm = pl.BlockSpec(memory_space=pl.ANY)
    n = len(arrays)
    return pl.pallas_call(
        hand_over_kernel,
        out_shape=tuple(jax.ShapeDtypeStruct(a.shape, a.dtype) for a in arrays),
        in_specs=[hbm] * n,
        out_specs=(hbm,) * n,
        scratch_shapes=[pltpu.VMEM(a.shape, a.dtype) for a in arrays]
        + [pltpu.SemaphoreType.DMA((2 * n,)), pltpu.SemaphoreType.DMA((2 * n,))],
    )(*arrays)


def shards(lookup_ids, bag_lengths, feature_widths, tables, w_in, w_out, cotangent):
    samples, bag = lookup_ids.shape[0], lookup_ids.shape[2]
    vocab = tables.shape[1]
    wide_in, hidden = w_in.shape
    wide_out = w_out.shape[1]
    in_rows, out_rows = wide_in // DEPTH, hidden // DEPTH
    half = samples // 2
    vmem = pl.BlockSpec(memory_space=pltpu.VMEM)
    hbm = pl.BlockSpec(memory_space=pl.ANY)
    dma = pltpu.SemaphoreType.DMA
    outs = pl.pallas_call(
        kernel,
        out_shape=(
            jax.ShapeDtypeStruct((samples, LANES), BF16),
            jax.ShapeDtypeStruct((in_rows, hidden), F32),
            jax.ShapeDtypeStruct((out_rows, wide_out), F32),
        ),
        in_specs=[pl.BlockSpec(memory_space=pltpu.SMEM), vmem, vmem, hbm, hbm, hbm, hbm],
        out_specs=(vmem, vmem, vmem),
        scratch_shapes=[
            pltpu.VMEM((vocab, LANES), BF16),
            pltpu.VMEM((wide_in, hidden), BF16),
            pltpu.VMEM((hidden, wide_out), BF16),
            pltpu.VMEM((samples, wide_out), BF16),
            pltpu.VMEM((samples, wide_in), BF16),
            pltpu.VMEM((samples, bag), jnp.int32),
            pltpu.VMEM((samples, 8), F32),
            pltpu.VMEM((2, samples // PIECES, vocab), BF16),
            pltpu.VMEM((samples, hidden), F32),
            pltpu.VMEM((samples, hidden), F32),
            pltpu.VMEM((samples, hidden), BF16),
            pltpu.VMEM((hidden, samples), BF16),
            pltpu.VMEM((samples, hidden), BF16),
            pltpu.VMEM((samples, wide_out), BF16),
            pltpu.VMEM((SIDE * SIDE, samples, LANES), BF16),
            pltpu.VMEM((2, 3, SIDE, half, LANES), BF16),
            pltpu.VMEM((2, 6, half, LANES), F32),
            pltpu.VMEM((2, SIDE, half, LANES), F32),
            pltpu.VMEM((9, in_rows, hidden), BF16),
            pltpu.VMEM((9, out_rows, wide_out), BF16),
            dma((4,)),
            dma((2,)),
            dma((32,)),
            dma((2,)),
            dma((13,)),
            dma((2,)),
            dma((21,)),
        ],
        compiler_params=pltpu.CompilerParams(
            collective_id=0, has_side_effects=True, vmem_limit_bytes=63 * 1024 * 1024
        ),
    )(
        feature_widths, jnp.transpose(lookup_ids[:, 0, :]), jnp.transpose(bag_lengths), tables[0], w_in, w_out, cotangent
    )
    return hand_over(outs)


def solution(mesh):
    return jax.shard_map(
        shards,
        mesh=mesh,
        in_specs=(
            P("dp", "table", None),
            P("dp", "table"),
            P(),
            P("table", None, "tensor"),
            P(None, ("table", "tensor")),
            P(("table", "tensor"), None),
            P("dp", ("table", "tensor")),
        ),
        out_specs=(
            P("dp", ("table", "tensor")),
            P("dp", ("table", "tensor")),
            P(("table", "tensor", "dp"), None),
        ),
        check_vma=False,
    )
```

time: 152 us -> 128 us (0.84)
  Pallas kernels: 142 us -> 127 us
  local copies, waits for them, and re-layouts: 9.23 us -> 0 us
    pallas_call x1, Pallas kernels: 142 us -> 125 us  [shards(): pl.pallas_call(kernel, out_shape=(jax.ShapeDtypeStruct((samples, LANES),...]
    unnamed x5 -> x0, local copies, waits for them, and re-layouts: 9.23 us -> none
    pallas_call x0 -> x1, Pallas kernels: none -> 2.54 us  [hand_over(): pl.pallas_call(hand_over_kernel, out_shape=tuple((jax.ShapeDtypeStruct(a....]
where the time goes in v2:
time: 128 us
  Pallas kernels  127 us (99%)
    pallas_call x1, Pallas kernels, shards(): pl.pallas_call(kernel, out_shape=(jax.ShapeDtypeStruct((samples, LANES),...  125 us

profile of v2, /device:TPU:1, one launch (start us, length us, event | category | flops | bytes accessed | tf_op | source)
XLA Modules:
  0.0 128.2 jit_solution(685131475843671252)
XLA Ops:
  0.6 124.8 %shard_map.94 = (bf16[512,128]{1,0:T(8,128)(2,1)}, f32[512,512]{1,0:T(8,128)}, f32[64,4096]{1,0:T(8,128)}) custom-call(s32[16]{0:T(128)} %widths.1, s32[16,512]{1,0:T(8,128)} %bitcast.6, s32[1,512]{1,0:T(1,128)} %bitcast.7, bf16[4096,128]{1,0:T(8,128)(2,1)} %bitcast.5, bf16[4096,512]{1,0:T(8,128)(2,1)} %w_in_hbm.1, bf16[512,4096]{1,0:T(8,128)(2,1)} %w_out_hbm.1, ...), custom_call_target="tpu_custom_call" | custom-call | tf_op jit(solution)/shard_map/pallas_call | solution.py:512
  125.5 2.5 %shard_map.95 = (bf16[512,128]{1,0:T(8,128)(2,1)}, f32[512,512]{1,0:T(8,128)}, f32[64,4096]{1,0:T(8,128)}) custom-call(bf16[512,128]{1,0:T(8,128)(2,1)} %get-tuple-element.6.refs_0_, f32[512,512]{1,0:T(8,128)} %get-tuple-element.7.refs_1_, f32[64,4096]{1,0:T(8,128)} %get-tuple-element.8.refs_2_), custom_call_target="tpu_custom_call" | custom-call | tf_op jit(solution)/shard_map/pallas_call | solution.py:492

commit v3 on v2

--- a/solution.py
+++ b/solution.py
@@ -25,10 +25,11 @@
 
 def kernel(
     widths, ids, lens, table_hbm, w_in_hbm, w_out_hbm, cot_hbm,
+    mixed_hbm, grad_in_hbm, grad_out_hbm,
     mixed, grad_in, grad_out,
     table, w_in, w_out, cot, feat, keys, spans, counts, gh, pre, hid, hid_t, gp,
     part, pair, st1, st2, row_sum, z_in, z_out,
-    in_sem, ag_send, ag_recv, rs_send, rs_recv, z_send, z_recv,
+    in_sem, out_sem, ag_send, ag_recv, rs_send, rs_recv, z_send, z_recv,
 ):
     t, yh, z = lax.axis_index("table"), lax.axis_index("tensor"), lax.axis_index("dp")
     core = lax.rem(t, 2)
@@ -75,6 +76,7 @@
     neighbours = [
         dev(ring(x + 1), y, core, z), dev(ring(x - 1), y, core, z),
         dev(x, ring(y + 1), core, z), dev(x, ring(y - 1), core, z),
+        dev(ring(x + 2), y, core, z), dev(x, ring(y + 2), core, z),
         dev(x, y, core, ring_z(z + 1)), dev(x, y, core, ring_z(z - 1)), partner,
     ]
     for neighbour in neighbours:
@@ -119,6 +121,7 @@
                 a, b = first[h], second[h]
                 copy(h, a, b, core, peer(h, ring(a + turn), b))
                 copy(h, a, b, 1 - core, peer(h, ring(a - turn), b))
+                copy(h, a, b, 2, peer(h, ring(a + 2), b))
             for h in range(2):
                 line(h, 0)
                 to_partner(h, first[h], second[h])
@@ -128,7 +131,6 @@
             for h in range(2):
                 a, b = first[h], second[h]
                 aj = ring(a - turn)
-                copy(h, aj, b, 2, peer(h, ring(a + turn), b))
                 line(h, 1)
                 to_partner(h, aj, b)
 
@@ -441,6 +443,8 @@
     z_step("in+", 2)
     z_step("in-", 2)
     rs_last()
+    mixed_out = pltpu.make_async_copy(mixed, mixed_hbm, out_sem.at[0])
+    mixed_out.start()
     z_step("out+", 3)
     z_step("in-", 3)
     add_in(z, [], grad_in, 0, in_rows)
@@ -450,18 +454,25 @@
     for n in range(2):
         z_copy("in+", 2, n).wait_recv()
     grad_in[...] += z_in[2].astype(F32)
+    leaving = [mixed_out]
     for n in range(2):
-        r = slice(n * in_half, (n + 1) * in_half)
+        r = pl.ds(n * in_half, in_half)
         z_copy("in-", 3, n).wait_recv()
         grad_in[r, :] += z_in[6, r].astype(F32)
+        leaving.append(pltpu.make_async_copy(grad_in.at[r], grad_in_hbm.at[r], out_sem.at[1 + n]))
+        leaving[-1].start()
     z_copy("out+", 3).wait_recv()
     grad_out[...] += z_out[3].astype(F32)
+    leaving.append(pltpu.make_async_copy(grad_out, grad_out_hbm, out_sem.at[3]))
+    leaving[-1].start()
     cot_sent()
     feat_sent()
     remote(part.at[:, : 18 * LANES], part.at[:, : 18 * LANES], rs_send.at[0], rs_recv.at[0], partner).wait_send()
     remote(pair, pair, rs_send.at[1], rs_recv.at[12], partner).wait_send()
     for i, slots in enumerate((z_in, z_out)):
         remote(slots.at[0:7], slots.at[0:7], z_send.at[i], z_recv.at[7 * i], up).wait_send()
+    for c in leaving:
+        c.wait()
 
 
 def hand_over_kernel(*refs):
@@ -517,8 +528,11 @@
             jax.ShapeDtypeStruct((out_rows, wide_out), F32),
         ),
         in_specs=[pl.BlockSpec(memory_space=pltpu.SMEM), vmem, vmem, hbm, hbm, hbm, hbm],
-        out_specs=(vmem, vmem, vmem),
+        out_specs=(hbm, hbm, hbm),
         scratch_shapes=[
+            pltpu.VMEM((samples, LANES), BF16),
+            pltpu.VMEM((in_rows, hidden), F32),
+            pltpu.VMEM((out_rows, wide_out), F32),
             pltpu.VMEM((vocab, LANES), BF16),
             pltpu.VMEM((wide_in, hidden), BF16),
             pltpu.VMEM((hidden, wide_out), BF16),
@@ -540,6 +554,7 @@
             pltpu.VMEM((9, in_rows, hidden), BF16),
             pltpu.VMEM((9, out_rows, wide_out), BF16),
             dma((4,)),
+            dma((4,)),
             dma((2,)),
             dma((32,)),
             dma((2,)),

time: 128 us -> 127 us (level)
  no operation moved by 1% of the time
where the time goes in v3:
time: 127 us
  Pallas kernels  126 us (99%)
    pallas_call x1, Pallas kernels, shards(): pl.pallas_call(kernel, out_shape=(jax.ShapeDtypeStruct((samples, LANES),...  124 us

profile of v3, /device:TPU:1, one launch (start us, length us, event | category | flops | bytes accessed | tf_op | source)
XLA Modules:
  0.0 127.1 jit_solution(8743563830637583796)
XLA Ops:
  0.6 123.7 %shard_map.94 = (bf16[512,128]{1,0:T(8,128)(2,1)}, f32[512,512]{1,0:T(8,128)}, f32[64,4096]{1,0:T(8,128)}) custom-call(s32[16]{0:T(128)} %widths.1, s32[16,512]{1,0:T(8,128)} %bitcast.6, s32[1,512]{1,0:T(1,128)} %bitcast.7, bf16[4096,128]{1,0:T(8,128)(2,1)} %bitcast.5, bf16[4096,512]{1,0:T(8,128)(2,1)} %w_in_hbm.1, bf16[512,4096]{1,0:T(8,128)(2,1)} %w_out_hbm.1, ...), custom_call_target="tpu_custom_call" | custom-call | tf_op jit(solution)/shard_map/pallas_call | solution.py:523
  124.4 2.5 %shard_map.95 = (bf16[512,128]{1,0:T(8,128)(2,1)}, f32[512,512]{1,0:T(8,128)}, f32[64,4096]{1,0:T(8,128)}) custom-call(bf16[512,128]{1,0:T(8,128)(2,1)} %get-tuple-element.6.refs_0_, f32[512,512]{1,0:T(8,128)} %get-tuple-element.7.refs_1_, f32[64,4096]{1,0:T(8,128)} %get-tuple-element.8.refs_2_), custom_call_target="tpu_custom_call" | custom-call | tf_op jit(solution)/shard_map/pallas_call | solution.py:503
